TPU v7x, 32 devices: a whole 2x2x4 slice. The times are simulated.
32 devices in a mesh: gx: 8 (over z, y), gy: 4 (over x, core).
Axes of the slice: x: 2, y: 2, z: 4, core: 2. Of those that a mesh axis runs over, the one named last changes fastest.
Arguments:
- populations: float32 [19, 64, 256, 128], P(None, 'gx', 'gy'), may hold values from 0.5 to 2
- solid_flags: int32 [64, 256, 128], P('gx', 'gy'), may hold values 0 or 1
- point_cells: int32 [3, 4608], replicated, may hold values from 0 to 255, as said below
- point_turbine: int32 [4608], replicated, may hold values from 0 to 23, as said below
- blade_speed: float32 [3, 4608], replicated, may hold values from -0.3 to 0.3
- chord: float32 [4608], replicated, may hold values from 0.3 to 3
- turbine_gain: float32 [24], replicated, may hold values from 0.5 to 2
Outputs:
- read: float32 [19, 64, 256, 128], P(None, 'gx', 'gy')
- point_force: float32 [3, 4608], replicated
Inputs may be any that keep to these rules, and one draw needn't show every extreme that they name: `point_cells`: row 0 and row 1 are a point's streamwise and spanwise cell, row 2 its height, which lies in [4, 124]; all points of one turbine share the streamwise cell. `point_turbine`: each turbine has exactly 192 points.
All inputs are finite; a program needn't handle non-finite values. No bound on the sum of `solid_flags` on one device may be relied on, other than what follows from the above.
Results may differ from a plain program's by a relative error of at most 0.00007.
Values sent between devices are 32-bit elements; how exact they have to be, the bound alone decides.
A program may use at most 128 MiB of HBM per device.

v0:
```python
import functools
import math

import jax
import jax.numpy as jnp
import numpy as np
from jax import lax
from jax.experimental import pallas as pl
from jax.experimental.pallas import tpu as pltpu
from jax.sharding import PartitionSpec as P

SMEAR = 3
lattice_dirs = [
    (0, 0, 0),
    (1, 0, 0),
    (-1, 0, 0),
    (0, 1, 0),
    (0, -1, 0),
    (0, 0, 1),
    (0, 0, -1),
    (1, 1, 0),
    (-1, -1, 0),
    (1, -1, 0),
    (-1, 1, 0),
    (1, 0, 1),
    (-1, 0, -1),
    (1, 0, -1),
    (-1, 0, 1),
    (0, 1, 1),
    (0, -1, -1),
    (0, 1, -1),
    (0, -1, 1),
]
opposite_dir = [0, 2, 1, 4, 3, 6, 5, 8, 7, 10, 9, 12, 11, 14, 13, 16, 15, 18, 17]
lattice_wts = [1.0 / 3.0] + [1.0 / 18.0] * 6 + [1.0 / 36.0] * 12
relax_time = 0.8
kernel_scale = 1.5
NDIR = 19
EAST = [k for k in range(NDIR) if lattice_dirs[k][0] == 1]
WEST = [k for k in range(NDIR) if lattice_dirs[k][0] == -1]
NORTH = [k for k in range(NDIR) if lattice_dirs[k][1] == 1]
SOUTH = [k for k in range(NDIR) if lattice_dirs[k][1] == -1]
CORNERS = [7, 8, 9, 10]
MESH = pl.DeviceIdType.MESH
f32 = jnp.float32
bf16 = jnp.bfloat16
NT = (((1,), (1,)), ((), ()))
VLIM = 48 * 1024 * 1024
SORT_CHUNK = 512


def split3(x):
    a = x.astype(bf16).astype(f32)
    r = x - a
    b = r.astype(bf16).astype(f32)
    return a, b, r - b


def iota(shape, dim):
    return lax.broadcasted_iota(jnp.int32, shape, dim)


def moments(g):
    side = g[1]
    for k in range(2, 7):
        side = side + g[k]
    diag = g[7]
    for k in range(8, 19):
        diag = diag + g[k]
    rho = g[0] * (1.0 / 3.0) + side * (1.0 / 18.0) + diag * (1.0 / 36.0)
    mom = []
    for axis in range(3):
        first, rest = None, None
        for k in range(1, 19, 2):
            step = lattice_dirs[k][axis]
            if step == 0:
                continue
            diff = g[k] - g[k + 1] if step == 1 else g[k + 1] - g[k]
            if k < 7:
                first = diff if first is None else first + diff
            else:
                rest = diff if rest is None else rest + diff
        mom.append(first * (1.0 / 18.0) + rest * (1.0 / 36.0))
    return rho, mom


def sample_kernel(
    turbines,
    hub_ref,
    cells_ref,
    turb_ref,
    blade_ref,
    chord_ref,
    gain_ref,
    pops_hbm,
    samp_ref,
    table_ref,
    rank_ref,
    pops,
    acc_ref,
    sems,
):
    wx, wy, nz = pops.shape[1:]
    points = turb_ref.shape[1]
    group = points // turbines
    start_x = lax.axis_index("gx") * wx
    start_y = lax.axis_index("gy") * wy

    def plane_copy(x):
        return pltpu.make_async_copy(pops_hbm.at[:, x], pops.at[:, x], sems.at[x])

    for x in range(wx):
        plane_copy(x).start()

    lanes = 128
    chunks = points // lanes
    hot = []
    for k in range(chunks):
        own = turb_ref[:, k * lanes : (k + 1) * lanes]
        hot.append((own == iota((turbines, lanes), 0)).astype(f32))
    stacked = jnp.concatenate(hot, axis=0).astype(bf16)
    upto = (iota((lanes, lanes), 0) <= iota((lanes, lanes), 1)).astype(bf16)
    inside = jnp.dot(stacked, upto, preferred_element_type=f32)
    whole = jnp.dot(stacked, jnp.ones((lanes, lanes), bf16), preferred_element_type=f32)
    before = jnp.full((turbines, lanes), -1.0, f32)
    for k in range(chunks):
        rows = slice(k * turbines, (k + 1) * turbines)
        rank = jnp.sum(hot[k] * (inside[rows] + before), axis=0, keepdims=True)
        rank_ref[:, k * lanes : (k + 1) * lanes] = rank
        before = before + whole[rows]

    acc_ref[...] = jnp.zeros_like(acc_ref)

    def sort_chunk(k, carry):
        cols = pl.ds(pl.multiple_of(k * SORT_CHUNK, SORT_CHUNK), SORT_CHUNK)
        mine = turb_ref[:, cols] == iota((turbines, SORT_CHUNK), 0)
        pos_y = cells_ref[1:2, cols].astype(f32)
        pos_z = cells_ref[2:3, cols].astype(f32)
        y_high = pos_y.astype(bf16).astype(f32)
        rows = [y_high, pos_y - y_high, pos_z]
        for c in range(3):
            rows += list(split3(blade_ref[c : c + 1, cols]))
        rows += list(split3(chord_ref[:, cols] * gain_ref[...]))
        data = jnp.concatenate([jnp.where(mine, r, 0.0) for r in rows], axis=0).astype(bf16)
        place = (rank_ref[:, cols] == iota((group, SORT_CHUNK), 0).astype(f32)).astype(f32)
        acc_ref[...] += lax.dot_general(
            data, place.astype(bf16), NT, preferred_element_type=f32
        )
        return carry

    lax.fori_loop(0, points // SORT_CHUNK, sort_chunk, 0)

    def part(j):
        return acc_ref[j * turbines : (j + 1) * turbines]

    table_ref[0:turbines] = part(0) + part(1)
    table_ref[turbines : 2 * turbines] = part(2)
    for q in range(4):
        at = 3 + 3 * q
        table_ref[(2 + q) * turbines : (3 + q) * turbines] = part(at) + part(at + 1) + part(at + 2)

    samp_ref[...] = jnp.zeros_like(samp_ref)
    for x in range(wx):
        plane_copy(x).wait()
    per = samp_ref.shape[1]

    def one_turbine(t, carry):
        lx = hub_ref[t] - start_x

        @pl.when((lx >= 0) & (lx < wx))
        def _():
            rho, mom = moments([pops[i, lx] for i in range(NDIR)])
            vel = jnp.concatenate([m / rho for m in mom], axis=0)
            split = jnp.concatenate(split3(vel), axis=0).astype(bf16)
            pos_y = table_ref[pl.ds(t, 1), :].astype(jnp.int32)
            pos_z = table_ref[pl.ds(turbines + t, 1), :].astype(jnp.int32)
            pick_z = (iota((nz, group), 0) == pos_z).astype(f32).astype(bf16)
            at_z = jnp.dot(split, pick_z, preferred_element_type=f32)
            n = 3 * wy
            at_z = at_z[:n] + at_z[n : 2 * n] + at_z[2 * n :]
            pick_y = iota((wy, group), 0) + start_y == pos_y
            for c in range(3):
                one = jnp.sum(
                    jnp.where(pick_y, at_z[c * wy : (c + 1) * wy], 0.0), axis=0, keepdims=True
                )
                row = c * turbines + t
                samp_ref[row // per, pl.ds(row % per, 1), :] = one

        return carry

    lax.fori_loop(0, turbines, one_turbine, 0)


def reduce_kernel(nx, ny, s_ref, out_ref, rx, ry, red, ss1, sr1, ss2, sr2, ss3, sr3):
    gx = lax.axis_index("gx")
    gy = lax.axis_index("gy")
    xs = [lax.rem(gx + k, nx) for k in range(nx)]
    ys = [lax.rem(gy + k, ny) for k in range(ny)]
    barrier = pltpu.get_barrier_semaphore()
    for k in range(1, nx):
        pl.semaphore_signal(barrier, inc=1, device_id=(xs[k], gy), device_id_type=MESH)
    for k in range(1, ny):
        pl.semaphore_signal(barrier, inc=1, device_id=(gx, ys[k]), device_id_type=MESH)
    pl.semaphore_wait(barrier, nx + ny - 2)

    first = []
    for k in range(1, nx):
        first.append(
            pltpu.make_async_remote_copy(
                src_ref=s_ref.at[xs[k]],
                dst_ref=rx.at[k],
                send_sem=ss1.at[k],
                recv_sem=sr1.at[k],
                device_id=(xs[k], gy),
                device_id_type=MESH,
            )
        )
        first[-1].start()
    total = s_ref[gx]
    for k in range(1, nx):
        first[k - 1].wait_recv()
        total = total + rx[k]
    red[...] = total

    second = []
    for k in range(1, ny):
        second.append(
            pltpu.make_async_remote_copy(
                src_ref=red,
                dst_ref=ry.at[k],
                send_sem=ss2.at[k],
                recv_sem=sr2.at[k],
                device_id=(gx, ys[k]),
                device_id_type=MESH,
            )
        )
        second[-1].start()
    for k in range(1, ny):
        second[k - 1].wait_recv()
        total = total + ry[k]
    out_ref[gx] = total

    third = []
    for k in range(1, nx):
        third.append(
            pltpu.make_async_remote_copy(
                src_ref=out_ref.at[gx],
                dst_ref=out_ref.at[gx],
                send_sem=ss3.at[k],
                recv_sem=sr3.at[k],
                device_id=(xs[k], gy),
                device_id_type=MESH,
            )
        )
        third[-1].start()
    for copy in first + second:
        copy.wait_send()
    for copy in third:
        copy.wait()


def wrapped(offset, total):
    offset = jnp.where(offset >= total // 2, offset - total, offset)
    return jnp.where(offset < -(total // 2), offset + total, offset)


def kernel_value(offset):
    dist = offset.astype(f32)
    return jnp.where(
        jnp.abs(offset) <= SMEAR, jnp.exp(-((dist / kernel_scale) ** 2)), jnp.float32(0.0)
    )


def collide_kernel(
    turbines,
    total_x,
    total_y,
    hub_ref,
    samp_ref,
    table_ref,
    solid_hbm,
    pops_hbm,
    pfs_ref,
    north_ref,
    south_ref,
    post_hbm,
    pops,
    solid,
    force,
    field,
    sems,
    out_sems,
):
    wx, wy, nz = pops.shape[1:]
    group = table_ref.shape[1]
    start_x = lax.axis_index("gx") * wx
    start_y = lax.axis_index("gy") * wy

    def plane_copy(x):
        return pltpu.make_async_copy(pops_hbm.at[:, x], pops.at[:, x], sems.at[x])

    def plane_out(x):
        return pltpu.make_async_copy(pops.at[:, x], post_hbm.at[:, x], out_sems.at[x])

    solid_copy = pltpu.make_async_copy(solid_hbm, solid, sems.at[wx])
    solid_copy.start()
    for x in range(wx):
        plane_copy(x).start()

    def rows(j):
        return table_ref[j * turbines : (j + 1) * turbines]

    rel = [samp_ref[c * turbines : (c + 1) * turbines] - rows(2 + c) for c in range(3)]
    speed = jnp.sqrt(rel[0] * rel[0] + rel[1] * rel[1] + rel[2] * rel[2] + 0.0001)
    scale = -(rows(5) * speed)
    for c in range(3):
        pfs_ref[c * turbines : (c + 1) * turbines] = scale * rel[c]

    force[...] = jnp.zeros_like(force)
    reach = [float(np.float32(math.exp(-((d / kernel_scale) ** 2)))) for d in range(SMEAR + 1)]

    def one_turbine(t, carry):
        hub = hub_ref[t]

        @pl.when(lax.rem(hub - start_x + SMEAR + total_x, total_x) < wx + 2 * SMEAR)
        def _():
            pos_y = table_ref[pl.ds(t, 1), :].astype(jnp.int32)
            pos_z = table_ref[pl.ds(turbines + t, 1), :].astype(jnp.int32)
            kern_y = kernel_value(wrapped(iota((wy, group), 0) + start_y - pos_y, total_y))
            kern_z = kernel_value(iota((nz, group), 0) - pos_z)
            left = jnp.concatenate(
                [kern_y * pfs_ref[pl.ds(c * turbines + t, 1), :] for c in range(3)], axis=0
            )
            field[...] = lax.dot_general(
                left, kern_z, NT, preferred_element_type=f32, precision=lax.Precision.HIGHEST
            )

            def one_plane(x, inner):
                away = jnp.abs(wrapped(start_x + x - hub, total_x))

                @pl.when(away <= SMEAR)
                def _():
                    kern_x = jnp.float32(reach[3])
                    for d in range(3):
                        kern_x = jnp.where(away == d, jnp.float32(reach[d]), kern_x)
                    for c in range(3):
                        force[c, x] += kern_x * field[c * wy : (c + 1) * wy]

                return inner

            lax.fori_loop(0, wx, one_plane, 0)

        return carry

    lax.fori_loop(0, turbines, one_turbine, 0)
    solid_copy.wait()
    step = 8

    def one_block(x, b):
        at = pl.ds(pl.multiple_of(b * step, step), step)
        g = [pops[i, x, at, :] for i in range(NDIR)]
        rho, mom = moments(g)
        frc = [force[c, x, at, :] for c in range(3)]
        inv = 1.0 / rho
        vel = [(mom[c] + 0.5 * frc[c]) * inv for c in range(3)]
        wall = solid[x, at, :] != 0
        usq = vel[0] * vel[0] + vel[1] * vel[1] + vel[2] * vel[2]
        uf = vel[0] * frc[0] + vel[1] * frc[1] + vel[2] * frc[2]
        om = 1.0 / relax_time
        pre = 1.0 - 0.5 / relax_time
        keep = 1.0 - om
        base = (om * rho) * (1.0 - 1.5 * usq) - (3.0 * pre) * uf
        quad = (4.5 * om) * rho
        lin = (3.0 * om) * rho
        pops[0, x, at, :] = jnp.where(wall, g[0], keep * g[0] + base)
        for k in range(1, NDIR, 2):
            cu, cf = None, None
            for axis in range(3):
                s = lattice_dirs[k][axis]
                if s == 0:
                    continue
                if cu is None:
                    cu, cf = (vel[axis], frc[axis]) if s == 1 else (-vel[axis], -frc[axis])
                elif s == 1:
                    cu, cf = cu + vel[axis], cf + frc[axis]
                else:
                    cu, cf = cu - vel[axis], cf - frc[axis]
            even = base + cu * (quad * cu + (9.0 * pre) * cf)
            odd = lin * cu + (3.0 * pre) * cf
            pops[k, x, at, :] = jnp.where(wall, g[k + 1], keep * g[k] + (even + odd))
            pops[k + 1, x, at, :] = jnp.where(wall, g[k], keep * g[k + 1] + (even - odd))

    def one_plane(x, carry):
        plane_copy(x).wait()

        def blocks(b, inner):
            one_block(x, b)
            return inner

        lax.fori_loop(0, wy // step, blocks, 0)
        for j, k in enumerate(NORTH):
            north_ref[j, pl.ds(x, 1), :] = pops[k, x, wy - 1 : wy, :]
        for j, k in enumerate(SOUTH):
            south_ref[j, pl.ds(x, 1), :] = pops[k, x, 0:1, :]

        @pl.when(x > 0)
        def _():
            plane_out(x - 1).start()

        return carry

    lax.fori_loop(0, wx, one_plane, 0)
    plane_out(wx - 1).start()
    for x in range(wx):
        plane_out(x).wait()


def halo_kernel(
    nx, ny, wx, post, north, south, from_w, from_e, from_s, from_n, from_c, send, recv
):
    gx = lax.axis_index("gx")
    gy = lax.axis_index("gy")
    east, west = lax.rem(gx + 1, nx), lax.rem(gx + nx - 1, nx)
    up, down = lax.rem(gy + 1, ny), lax.rem(gy + ny - 1, ny)
    barrier = pltpu.get_barrier_semaphore()
    near = [
        (east, gy), (west, gy), (gx, up), (gx, down),
        (east, up), (west, down), (east, down), (west, up),
    ]
    for dev in near:
        pl.semaphore_signal(barrier, inc=1, device_id=dev, device_id_type=MESH)
    pl.semaphore_wait(barrier, len(near))
    moves = []
    for j, k in enumerate(EAST):
        moves.append((post.at[k, wx - 1], from_w.at[j], (east, gy)))
    for j, k in enumerate(WEST):
        moves.append((post.at[k, 0], from_e.at[j], (west, gy)))
    moves.append((north, from_s, (gx, up)))
    moves.append((south, from_n, (gx, down)))
    for j, k in enumerate(CORNERS):
        side = north if k in NORTH else south
        ids = NORTH if k in NORTH else SOUTH
        moves.append((side.at[ids.index(k)], from_c.at[j], near[4 + j]))
    copies = []
    for n, (src, dst, dev) in enumerate(moves):
        copies.append(
            pltpu.make_async_remote_copy(
                src_ref=src,
                dst_ref=dst,
                send_sem=send.at[n],
                recv_sem=recv.at[n],
                device_id=dev,
                device_id_type=MESH,
            )
        )
        copies[-1].start()
    for copy in copies:
        copy.wait()


def stream_kernel(
    post_hbm, from_w, from_e, from_s, from_n, from_c, out_hbm, held, rows, outs, sems, out_sems
):
    wx = post_hbm.shape[1]
    wy, nz = post_hbm.shape[2:]

    def plane_in(x):
        return pltpu.make_async_copy(post_hbm.at[:, x], held.at[:, x + 1], sems.at[x])

    def plane_out(x):
        return pltpu.make_async_copy(outs.at[:, x], out_hbm.at[:, x], out_sems.at[x])

    for x in range(wx):
        plane_in(x).start()
    edge = 8
    for j, k in enumerate(EAST):
        held[k, 0] = from_w[j]
    for j, k in enumerate(WEST):
        held[k, wx + 1] = from_e[j]
    for ids, src, at in ((NORTH, from_s, 0), (SOUTH, from_n, 5)):
        for j, k in enumerate(ids):
            rows[at + j, edge : edge + wx, :] = src[j]
            if k in CORNERS:
                n = CORNERS.index(k)
                if lattice_dirs[k][0] == 1:
                    rows[at + j, edge - 1 : edge, :] = from_c[n, wx - 1 : wx, :]
                else:
                    rows[at + j, edge + wx : edge + wx + 1, :] = from_c[n, 0:1, :]
    plane_in(0).wait()
    row_at = iota((wy, nz), 0)
    lane_at = iota((wy, nz), 1)

    def one_plane(x, carry):
        @pl.when(x < wx - 1)
        def _():
            plane_in(x + 1).wait()

        for i in range(NDIR):
            sx, sy, sz = lattice_dirs[i]
            val = held[i, x + 1 - sx]
            if sy:
                line = (NORTH.index(i)) if sy == 1 else 5 + SOUTH.index(i)
                fill = rows[line, pl.ds(edge + x - sx, 1), :]
                val = pltpu.roll(val, sy % wy, 0)
                val = jnp.where(row_at == (0 if sy == 1 else wy - 1), fill, val)
            if sz:
                val = pltpu.roll(val, sz % nz, 1)
                mirror = held[opposite_dir[i], x + 1]
                val = jnp.where(lane_at == (0 if sz == 1 else nz - 1), mirror, val)
            outs[i, x] = val

        @pl.when(x > 0)
        def _():
            plane_out(x - 1).start()

        return carry

    lax.fori_loop(0, wx, one_plane, 0)
    plane_out(wx - 1).start()
    for x in range(wx):
        plane_out(x).wait()


def unsort_kernel(turbines, turb_ref, rank_ref, pfs_ref, out_ref):
    group = pfs_ref.shape[1]
    points = turb_ref.shape[1]
    data = jnp.concatenate(split3(pfs_ref[...]), axis=0).astype(bf16)
    n = 3 * turbines

    def chunk(k, carry):
        cols = pl.ds(pl.multiple_of(k * SORT_CHUNK, SORT_CHUNK), SORT_CHUNK)
        mine = turb_ref[:, cols] == iota((turbines, SORT_CHUNK), 0)
        place = (rank_ref[:, cols] == iota((group, SORT_CHUNK), 0).astype(f32)).astype(f32)
        got = jnp.dot(data, place.astype(bf16), preferred_element_type=f32)
        got = got[:n] + got[n : 2 * n] + got[2 * n :]
        for c in range(3):
            out_ref[c : c + 1, cols] = jnp.sum(
                jnp.where(mine, got[c * turbines : (c + 1) * turbines], 0.0), axis=0, keepdims=True
            )
        return carry

    lax.fori_loop(0, points // SORT_CHUNK, chunk, 0)


def body(populations, solid_flags, point_cells, point_turbine, blade_speed, chord, turbine_gain):
    wx, wy, nz = populations.shape[1:]
    nx, ny = lax.axis_size("gx"), lax.axis_size("gy")
    turbines = turbine_gain.shape[0]
    points = point_turbine.shape[0]
    group = points // turbines
    vmem = pl.BlockSpec(memory_space=pltpu.VMEM)
    smem = pl.BlockSpec(memory_space=pltpu.SMEM)
    hbm = pl.BlockSpec(memory_space=pl.ANY)
    shape = jax.ShapeDtypeStruct
    params = pltpu.CompilerParams(vmem_limit_bytes=VLIM)
    onehot = point_turbine[None, :] == jnp.arange(turbines, dtype=jnp.int32)[:, None]
    hubs = jnp.max(jnp.where(onehot, point_cells[0][None, :], 0), axis=1)
    turb = point_turbine.reshape(1, points)
    dma = pltpu.SemaphoreType.DMA
    per = -(-3 * turbines // (8 * nx)) * 8

    samples, table, rank = pl.pallas_call(
        functools.partial(sample_kernel, turbines),
        out_shape=(
            shape((nx, per, group), f32),
            shape((6 * turbines, group), f32),
            shape((1, points), f32),
        ),
        in_specs=[smem, vmem, vmem, vmem, vmem, vmem, hbm],
        out_specs=(vmem, vmem, vmem),
        scratch_shapes=[
            pltpu.VMEM(populations.shape, f32),
            pltpu.VMEM((15 * turbines, group), f32),
            dma((wx,)),
        ],
        compiler_params=params,
        name="sample",
    )(
        hubs,
        point_cells,
        turb,
        blade_speed,
        chord.reshape(1, points),
        turbine_gain.reshape(turbines, 1),
        populations,
    )

    summed = pl.pallas_call(
        functools.partial(reduce_kernel, nx, ny),
        out_shape=shape((nx, per, group), f32),
        in_specs=[vmem],
        out_specs=vmem,
        scratch_shapes=[
            pltpu.VMEM((nx, per, group), f32),
            pltpu.VMEM((ny, per, group), f32),
            pltpu.VMEM((per, group), f32),
            dma((nx,)),
            dma((nx,)),
            dma((ny,)),
            dma((ny,)),
            dma((nx,)),
            dma((nx,)),
        ],
        compiler_params=pltpu.CompilerParams(collective_id=0, has_side_effects=True),
        name="reduce",
    )(samples)

    pfs, north, south, post = pl.pallas_call(
        functools.partial(collide_kernel, turbines, wx * nx, wy * ny),
        out_shape=(
            shape((3 * turbines, group), f32),
            shape((5, wx, nz), f32),
            shape((5, wx, nz), f32),
            shape(populations.shape, f32),
        ),
        in_specs=[smem, vmem, vmem, hbm, hbm],
        out_specs=(vmem, vmem, vmem, hbm),
        scratch_shapes=[
            pltpu.VMEM(populations.shape, f32),
            pltpu.VMEM((wx, wy, nz), jnp.int32),
            pltpu.VMEM((3, wx, wy, nz), f32),
            pltpu.VMEM((3 * wy, nz), f32),
            dma((wx + 1,)),
            dma((wx,)),
        ],
        compiler_params=params,
        name="collide",
    )(hubs, summed.reshape(nx * per, group), table, solid_flags, populations)

    halos = pl.pallas_call(
        functools.partial(halo_kernel, nx, ny, wx),
        out_shape=(
            shape((5, wy, nz), f32),
            shape((5, wy, nz), f32),
            shape((5, wx, nz), f32),
            shape((5, wx, nz), f32),
            shape((4, wx, nz), f32),
        ),
        in_specs=[hbm, vmem, vmem],
        out_specs=(vmem,) * 5,
        scratch_shapes=[dma((16,)), dma((16,))],
        compiler_params=pltpu.CompilerParams(collective_id=1, has_side_effects=True),
        name="halo",
    )(post, north, south)

    out = pl.pallas_call(
        stream_kernel,
        out_shape=shape(populations.shape, f32),
        in_specs=[hbm] + [vmem] * 5,
        out_specs=hbm,
        scratch_shapes=[
            pltpu.VMEM((NDIR, wx + 2, wy, nz), f32),
            pltpu.VMEM((10, wx + 16, nz), f32),
            pltpu.VMEM(populations.shape, f32),
            dma((wx,)),
            dma((wx,)),
        ],
        compiler_params=params,
        name="stream",
    )(post, *halos)

    point_force = pl.pallas_call(
        functools.partial(unsort_kernel, turbines),
        out_shape=shape((3, points), f32),
        in_specs=[vmem, vmem, vmem],
        out_specs=vmem,
        compiler_params=params,
        name="unsort",
    )(turb, rank, pfs)
    return out, point_force


def solution(mesh):
    in_specs = (P(None, "gx", "gy", None), P("gx", "gy", None), P(), P(), P(), P(), P())
    out_specs = (P(None, "gx", "gy", None), P())
    return jax.shard_map(body, mesh=mesh, in_specs=in_specs, out_specs=out_specs, check_vma=False)
```

profile of v0, /device:TPU:0, one launch (start us, length us, event | category | flops | bytes accessed | tf_op | source)
XLA Modules:
  0.0 72.7 jit_solution(16990932359646975888)
XLA Ops:
  0.6 0.7 %copy.10.gain_ref = f32[24,1]{1,0:T(8,128)S(1)} copy(f32[24,1]{0,1:T(1,128)} %bitcast.3) | data formatting | bytes 192 | tf_op jit(solution)/shard_map/reshape | solution.py:584
  1.4 0.7 %broadcast_in_dim.21.turb_ref = s32[1,4608]{1,0:T(1,128)S(1)} reshape(s32[4608]{0:T(1024)} %param.10) | data formatting | bytes 36864 | tf_op jit(solution)/shard_map/broadcast_in_dim | solution.py:556
  2.1 0.7 %reshape.15.chord_ref = f32[1,4608]{1,0:T(1,128)S(1)} reshape(f32[4608]{0:T(1024)} %param.12) | data formatting | bytes 36864 | tf_op jit(solution)/shard_map/reshape | solution.py:583
  2.9 0.9 %slice_reduce_fusion = s32[4608]{0:T(1024)S(1)} fusion(s32[3,4608]{1,0:T(4,128)} %cells_ref.1), kind=kLoop, calls=%fused_computation.2 | loop fusion | bytes 36864 | tf_op jit(solution)/shard_map/slice | solution.py:557
  3.8 0.9 %select_reduce_fusion.hub_ref = s32[24]{0:T(128)S(1)} fusion(s32[4608]{0:T(1024)S(1)} %slice_reduce_fusion, s32[4608]{0:T(1024)} %param.10), kind=kLoop, calls=%fused_computation | loop fusion | flops 331752 | bytes 36960 | tf_op jit(solution)/shard_map/reduce_max | solution.py:557
  4.7 0.0 copy-start.2
  4.7 2.4 %copy-done.2 = f32[19,8,64,128]{3,2,1,0:T(8,128)S(1)} copy-done((f32[19,8,64,128]{3,2,1,0:T(8,128)S(1)}, f32[19,8,64,128]{3,2,1,0:T(8,128)}, u32[]{:S(2)}) %copy-start.2) | copy-done | bytes 4980760
  7.1 0.0 copy-start.8
  7.1 0.9 %copy-done.8 = s32[3,4608]{1,0:T(4,128)S(1)} copy-done((s32[3,4608]{1,0:T(4,128)S(1)}, s32[3,4608]{1,0:T(4,128)}, u32[]{:S(2)}) %copy-start.8) | copy-done | bytes 55320
  8.0 0.0 copy-start.9
  8.0 0.9 %copy-done.9 = f32[3,4608]{1,0:T(4,128)S(1)} copy-done((f32[3,4608]{1,0:T(4,128)S(1)}, f32[3,4608]{1,0:T(4,128)}, u32[]{:S(2)}) %copy-start.9) | copy-done | bytes 55320
  8.9 0.0 copy-start.4
  8.9 4.7 %sample.1 = (f32[8,16,192]{2,1,0:T(8,128)S(1)}, f32[144,192]{1,0:T(8,128)S(1)}, f32[1,4608]{1,0:T(1,128)S(1)}) custom-call(s32[24]{0:T(128)S(1)} %select_reduce_fusion.hub_ref, s32[3,4608]{1,0:T(4,128)S(1)} %copy-done.8, s32[1,4608]{1,0:T(1,128)S(1)} %broadcast_in_dim.21.turb_ref, f32[3,4608]{1,0:T(4,128)S(1)} %copy-done.9, ...), custom_call_target="tpu_custom_call" | custom-call | tf_op jit(solution)/shard_map/sample/pallas_call | solution.py:562
  13.6 0.0 copy-start.7
  13.6 0.6 copy-done.7
  14.3 21.3 %reduce.3 = f32[8,16,192]{2,1,0:T(8,128)} custom-call(f32[8,16,192]{2,1,0:T(8,128)} %copy-done.7), custom_call_target="tpu_custom_call" | custom-call | tf_op jit(solution)/shard_map/reduce/pallas_call | solution.py:588
  35.6 0.0 copy-done.4
  35.6 0.0 copy-start.3
  35.6 0.9 %copy-done.3 = f32[8,16,192]{2,1,0:T(8,128)S(1)} copy-done((f32[8,16,192]{2,1,0:T(8,128)S(1)}, f32[8,16,192]{2,1,0:T(8,128)}, u32[]{:S(2)}) %copy-start.3) | copy-done | bytes 98328
  36.5 8.1 %collide.1 = (f32[72,192]{1,0:T(8,128)S(1)}, f32[5,8,128]{2,1,0:T(8,128)S(1)}, f32[5,8,128]{2,1,0:T(8,128)S(1)}, f32[19,8,64,128]{3,2,1,0:T(8,128)S(1)}) custom-call(s32[24]{0:T(128)S(1)} %select_reduce_fusion.hub_ref, f32[128,192]{1,0:T(8,128)S(1)} %bitcast.2, f32[144,192]{1,0:T(8,128)S(1)} %get-tuple-element.15.table_ref, s32[8,64,128]{2,1,0:T(8,128)S(1)} %copy-done.4, ...), custom_call_target="tpu_custom_call" | custom-call | tf_op jit(solution)/shard_map/collide/pallas_call | solution.py:608
  44.6 0.0 copy-start
  44.6 2.3 %copy-done = f32[19,8,64,128]{3,2,1,0:T(8,128)} copy-done((f32[19,8,64,128]{3,2,1,0:T(8,128)}, f32[19,8,64,128]{3,2,1,0:T(8,128)S(1)}, u32[]{:S(2)}) %copy-start) | copy-done | bytes 4980760
  46.9 0.0 copy-start.10
  46.9 0.6 copy-done.10
  47.5 0.0 copy-start.11
  47.5 0.6 copy-done.11
  48.1 2.8 %unsort.1 = f32[3,4608]{1,0:T(4,128)} custom-call(s32[1,4608]{1,0:T(1,128)S(1)} %broadcast_in_dim.21.turb_ref, f32[1,4608]{1,0:T(1,128)S(1)} %get-tuple-element.24.rank_ref, f32[72,192]{1,0:T(8,128)S(1)} %get-tuple-element.25.pfs_ref), custom_call_target="tpu_custom_call" | custom-call | tf_op jit(solution)/shard_map/unsort/pallas_call | solution.py:662
  50.8 12.3 %halo.1 = (f32[5,64,128]{2,1,0:T(8,128)}, f32[5,64,128]{2,1,0:T(8,128)}, f32[5,8,128]{2,1,0:T(8,128)}, f32[5,8,128]{2,1,0:T(8,128)}, f32[4,8,128]{2,1,0:T(8,128)}) custom-call(f32[19,8,64,128]{3,2,1,0:T(8,128)} %copy-done, f32[5,8,128]{2,1,0:T(8,128)} %copy-done.10, f32[5,8,128]{2,1,0:T(8,128)} %copy-done.11), custom_call_target="tpu_custom_call" | custom-call | tf_op jit(solution)/shard_map/halo/pallas_call | solution.py:630
  63.2 0.0 copy-start.1
  63.2 2.4 %copy-done.1 = f32[19,8,64,128]{3,2,1,0:T(8,128)S(1)} copy-done((f32[19,8,64,128]{3,2,1,0:T(8,128)S(1)}, f32[19,8,64,128]{3,2,1,0:T(8,128)}, u32[]{:S(2)}) %copy-start.1) | copy-done | bytes 4980760
  65.6 0.0 copy-start.5
  65.6 0.9 %copy-done.5 = f32[5,64,128]{2,1,0:T(8,128)S(1)} copy-done((f32[5,64,128]{2,1,0:T(8,128)S(1)}, f32[5,64,128]{2,1,0:T(8,128)}, u32[]{:S(2)}) %copy-start.5) | copy-done | bytes 163864
  66.5 0.0 copy-start.6
  66.5 0.9 %copy-done.6 = f32[5,64,128]{2,1,0:T(8,128)S(1)} copy-done((f32[5,64,128]{2,1,0:T(8,128)S(1)}, f32[5,64,128]{2,1,0:T(8,128)}, u32[]{:S(2)}) %copy-start.6) | copy-done | bytes 163864
  67.4 0.0 copy-start.12
  67.4 0.7 copy-done.12
  68.2 0.0 copy-start.13
  68.2 0.7 copy-done.13
  68.9 0.0 copy-start.14
  68.9 0.7 copy-done.14
  69.6 3.1 %stream.1 = f32[19,8,64,128]{3,2,1,0:T(8,128)} custom-call(f32[19,8,64,128]{3,2,1,0:T(8,128)S(1)} %copy-done.1, f32[5,64,128]{2,1,0:T(8,128)S(1)} %copy-done.5, f32[5,64,128]{2,1,0:T(8,128)S(1)} %copy-done.6, f32[5,8,128]{2,1,0:T(8,128)S(1)} %copy-done.12, f32[5,8,128]{2,1,0:T(8,128)S(1)} %copy-done.13, f32[4,8,128]{2,1,0:T(8,128)S(1)} %copy-done.14), custom_call_target="tpu_custom_call" | custom-call | tf_op jit(solution)/shard_map/stream/pallas_call | solution.py:646
Async XLA Ops:
  4.7 2.4 %copy-start.2 = (f32[19,8,64,128]{3,2,1,0:T(8,128)S(1)}, f32[19,8,64,128]{3,2,1,0:T(8,128)}, u32[]{:S(2)}) copy-start(f32[19,8,64,128]{3,2,1,0:T(8,128)} %pops_hbm.3) | copy-start | bytes 14942212
  7.1 0.9 %copy-start.8 = (s32[3,4608]{1,0:T(4,128)S(1)}, s32[3,4608]{1,0:T(4,128)}, u32[]{:S(2)}) copy-start(s32[3,4608]{1,0:T(4,128)} %cells_ref.1) | copy-start | bytes 165892
  8.0 0.9 %copy-start.9 = (f32[3,4608]{1,0:T(4,128)S(1)}, f32[3,4608]{1,0:T(4,128)}, u32[]{:S(2)}) copy-start(f32[3,4608]{1,0:T(4,128)} %blade_ref.1) | copy-start | bytes 165892
  8.9 26.7 %copy-start.4 = (s32[8,64,128]{2,1,0:T(8,128)S(1)}, s32[8,64,128]{2,1,0:T(8,128)}, u32[]{:S(2)}) copy-start(s32[8,64,128]{2,1,0:T(8,128)} %solid_hbm.1) | copy-start | bytes 786436
  13.6 0.7 copy-start.7
  35.6 0.9 %copy-start.3 = (f32[8,16,192]{2,1,0:T(8,128)S(1)}, f32[8,16,192]{2,1,0:T(8,128)}, u32[]{:S(2)}) copy-start(f32[8,16,192]{2,1,0:T(8,128)} %reduce.3) | copy-start | bytes 294916
  44.6 2.3 %copy-start = (f32[19,8,64,128]{3,2,1,0:T(8,128)}, f32[19,8,64,128]{3,2,1,0:T(8,128)S(1)}, u32[]{:S(2)}) copy-start(f32[19,8,64,128]{3,2,1,0:T(8,128)S(1)} %get-tuple-element.16.post.post_hbm) | copy-start | bytes 14942212
  46.9 0.6 copy-start.10
  47.5 0.6 copy-start.11
  63.2 2.4 %copy-start.1 = (f32[19,8,64,128]{3,2,1,0:T(8,128)S(1)}, f32[19,8,64,128]{3,2,1,0:T(8,128)}, u32[]{:S(2)}) copy-start(f32[19,8,64,128]{3,2,1,0:T(8,128)} %copy-done) | copy-start | bytes 14942212
  65.6 0.9 %copy-start.5 = (f32[5,64,128]{2,1,0:T(8,128)S(1)}, f32[5,64,128]{2,1,0:T(8,128)}, u32[]{:S(2)}) copy-start(f32[5,64,128]{2,1,0:T(8,128)} %get-tuple-element.19.from_w) | copy-start | bytes 491524
  66.5 0.9 %copy-start.6 = (f32[5,64,128]{2,1,0:T(8,128)S(1)}, f32[5,64,128]{2,1,0:T(8,128)}, u32[]{:S(2)}) copy-start(f32[5,64,128]{2,1,0:T(8,128)} %get-tuple-element.20.from_e) | copy-start | bytes 491524
  67.4 0.7 %copy-start.12 = (f32[5,8,128]{2,1,0:T(8,128)S(1)}, f32[5,8,128]{2,1,0:T(8,128)}, u32[]{:S(2)}) copy-start(f32[5,8,128]{2,1,0:T(8,128)} %get-tuple-element.21.from_s) | copy-start | bytes 61444
  68.2 0.7 %copy-start.13 = (f32[5,8,128]{2,1,0:T(8,128)S(1)}, f32[5,8,128]{2,1,0:T(8,128)}, u32[]{:S(2)}) copy-start(f32[5,8,128]{2,1,0:T(8,128)} %get-tuple-element.22.from_n) | copy-start | bytes 61444
  68.9 0.7 copy-start.14
where the time goes:
time: 73.8 us; the launch traced here: 72.7 us
  Pallas kernels  52.3 us (71%)
  local copies, waits for them, and re-layouts  18.8 us (25%)
  other arithmetic  0.9 us (1%)
    pallas_call x1, Pallas kernels, body(): pl.pallas_call(functools.partial(reduce_kernel, nx, ny), out_shape=shape(...  21.3 us
    unnamed x30, local copies, waits for them, and re-layouts  15.6 us
    pallas_call x1, Pallas kernels, body(): pl.pallas_call(functools.partial(halo_kernel, nx, ny, wx), out_shape=(sha...  12.3 us
    pallas_call x1, Pallas kernels, body(): pl.pallas_call(functools.partial(collide_kernel, turbines, wx * nx, wy *...  8.05 us
    pallas_call x1, Pallas kernels, body(): pl.pallas_call(functools.partial(sample_kernel, turbines), out_shape=(sha...  4.74 us
    pallas_call x1, Pallas kernels, body(): pl.pallas_call(stream_kernel, out_shape=shape(populations.shape, f32), in...  3.07 us
    pallas_call x1, Pallas kernels, body(): pl.pallas_call(functools.partial(unsort_kernel, turbines), out_shape=shap...  2.77 us

commit v1 on v0

--- a/solution.py
+++ b/solution.py
@@ -45,7 +45,8 @@
 f32 = jnp.float32
 bf16 = jnp.bfloat16
 NT = (((1,), (1,)), ((), ()))
-VLIM = 48 * 1024 * 1024
+VLIM = 67043328 - 0 * 1024
+STREAM_VLIM = 67043328 - 0 * 1024
 SORT_CHUNK = 512
 
 
@@ -84,24 +85,65 @@
     return rho, mom
 
 
+LANES = 128
+
+
+def fold_sizes(rows, group):
+    rest = group % LANES
+    half = -(-rows // 16) * 8 if 0 < rest <= LANES // 2 else 0
+    total = rows * (group // LANES) + (half or (rows if rest else 0))
+    return rest, half, total
+
+
+def folded(x):
+    rows, group = x.shape
+    rest, half, _ = fold_sizes(rows, group)
+    blocks = [x[:, i * LANES : (i + 1) * LANES] for i in range(group // LANES)]
+    if rest:
+        tail = x[:, group - rest :]
+        if half:
+            low = jnp.zeros((2 * half - rows, rest), f32)
+            second = jnp.concatenate([tail[half:], low], axis=0) if low.shape[0] else tail[half:]
+            tail = jnp.concatenate([tail[:half], second], axis=1)
+        width = tail.shape[1]
+        if width < LANES:
+            tail = jnp.concatenate([tail, jnp.zeros((tail.shape[0], LANES - width), f32)], axis=1)
+        blocks.append(tail)
+    return blocks
+
+
+def unfolded(flat, rows, group):
+    rest, half, _ = fold_sizes(rows, group)
+    n = group // LANES
+    blocks = [flat[i * rows : (i + 1) * rows] for i in range(n)]
+    if rest:
+        if half:
+            tail = flat[n * rows : n * rows + half]
+            second = tail[: rows - half, rest : 2 * rest]
+            blocks.append(jnp.concatenate([tail[:, :rest], second], axis=0))
+        else:
+            blocks.append(flat[n * rows : (n + 1) * rows, :rest])
+    return jnp.concatenate(blocks, axis=1)
+
+
 def sample_kernel(
     turbines,
-    hub_ref,
-    cells_ref,
-    turb_ref,
-    blade_ref,
-    chord_ref,
     gain_ref,
+    pack_ref,
     pops_hbm,
-    samp_ref,
+    flat_hbm,
     table_ref,
     rank_ref,
+    hubs_ref,
     pops,
     acc_ref,
+    samp_ref,
+    flat_ref,
+    hub_ref,
     sems,
 ):
     wx, wy, nz = pops.shape[1:]
-    points = turb_ref.shape[1]
+    points = pack_ref.shape[1]
     group = points // turbines
     start_x = lax.axis_index("gx") * wx
     start_y = lax.axis_index("gy") * wy
@@ -115,9 +157,19 @@
     lanes = 128
     chunks = points // lanes
     hot = []
+    hubs = jnp.zeros((turbines, lanes), f32)
     for k in range(chunks):
-        own = turb_ref[:, k * lanes : (k + 1) * lanes]
-        hot.append((own == iota((turbines, lanes), 0)).astype(f32))
+        own = pack_ref[0:1, k * lanes : (k + 1) * lanes]
+        hot.append((own == iota((turbines, lanes), 0).astype(f32)).astype(f32))
+        hubs = jnp.maximum(hubs, hot[k] * pack_ref[1:2, k * lanes : (k + 1) * lanes])
+    hubs_ref[...] = jnp.broadcast_to(
+        jnp.max(hubs, axis=1, keepdims=True), (turbines, lanes)
+    ).astype(jnp.int32)
+    hub_copy = pltpu.make_async_copy(hubs_ref, hub_ref, sems.at[wx])
+    hub_copy.start()
+    gain = jnp.zeros((turbines, 1), f32)
+    for t in range(turbines):
+        gain = jnp.where(iota((turbines, 1), 0) == t, gain_ref[t], gain)
     stacked = jnp.concatenate(hot, axis=0).astype(bf16)
     upto = (iota((lanes, lanes), 0) <= iota((lanes, lanes), 1)).astype(bf16)
     inside = jnp.dot(stacked, upto, preferred_element_type=f32)
@@ -133,14 +185,14 @@
 
     def sort_chunk(k, carry):
         cols = pl.ds(pl.multiple_of(k * SORT_CHUNK, SORT_CHUNK), SORT_CHUNK)
-        mine = turb_ref[:, cols] == iota((turbines, SORT_CHUNK), 0)
-        pos_y = cells_ref[1:2, cols].astype(f32)
-        pos_z = cells_ref[2:3, cols].astype(f32)
+        mine = pack_ref[0:1, cols] == iota((turbines, SORT_CHUNK), 0).astype(f32)
+        pos_y = pack_ref[2:3, cols]
+        pos_z = pack_ref[3:4, cols]
         y_high = pos_y.astype(bf16).astype(f32)
         rows = [y_high, pos_y - y_high, pos_z]
         for c in range(3):
-            rows += list(split3(blade_ref[c : c + 1, cols]))
-        rows += list(split3(chord_ref[:, cols] * gain_ref[...]))
+            rows += list(split3(pack_ref[4 + c : 5 + c, cols]))
+        rows += list(split3(pack_ref[7:8, cols] * gain))
         data = jnp.concatenate([jnp.where(mine, r, 0.0) for r in rows], axis=0).astype(bf16)
         place = (rank_ref[:, cols] == iota((group, SORT_CHUNK), 0).astype(f32)).astype(f32)
         acc_ref[...] += lax.dot_general(
@@ -162,10 +214,10 @@
     samp_ref[...] = jnp.zeros_like(samp_ref)
     for x in range(wx):
         plane_copy(x).wait()
-    per = samp_ref.shape[1]
+    hub_copy.wait()
 
     def one_turbine(t, carry):
-        lx = hub_ref[t] - start_x
+        lx = hub_ref[t, 0] - start_x
 
         @pl.when((lx >= 0) & (lx < wx))
         def _():
@@ -183,15 +235,23 @@
                 one = jnp.sum(
                     jnp.where(pick_y, at_z[c * wy : (c + 1) * wy], 0.0), axis=0, keepdims=True
                 )
-                row = c * turbines + t
-                samp_ref[row // per, pl.ds(row % per, 1), :] = one
+                samp_ref[pl.ds(c * turbines + t, 1), :] = one
 
         return carry
 
     lax.fori_loop(0, turbines, one_turbine, 0)
-
-
-def reduce_kernel(nx, ny, s_ref, out_ref, rx, ry, red, ss1, sr1, ss2, sr2, ss3, sr3):
+    blocks = folded(samp_ref[...])
+    flat_ref[...] = jnp.zeros_like(flat_ref)
+    at = 0
+    for block in blocks:
+        flat_ref[at : at + block.shape[0]] = block
+        at += block.shape[0]
+    out_copy = pltpu.make_async_copy(flat_ref, flat_hbm, sems.at[wx])
+    out_copy.start()
+    out_copy.wait()
+
+
+def reduce_kernel(nx, ny, s_ref, out_ref, mine, rx, ry, red, ss1, sr1, ss2, sr2, ss3, sr3):
     gx = lax.axis_index("gx")
     gy = lax.axis_index("gy")
     xs = [lax.rem(gx + k, nx) for k in range(nx)]
@@ -216,7 +276,10 @@
             )
         )
         first[-1].start()
-    total = s_ref[gx]
+    own = pltpu.make_async_copy(s_ref.at[gx], mine, sr1.at[0])
+    own.start()
+    own.wait()
+    total = mine[...]
     for k in range(1, nx):
         first[k - 1].wait_recv()
         total = total + rx[k]
@@ -238,13 +301,14 @@
     for k in range(1, ny):
         second[k - 1].wait_recv()
         total = total + ry[k]
-    out_ref[gx] = total
-
+    mine[...] = total
+    keep = pltpu.make_async_copy(mine, out_ref.at[gx], ss1.at[0])
+    keep.start()
     third = []
     for k in range(1, nx):
         third.append(
             pltpu.make_async_remote_copy(
-                src_ref=out_ref.at[gx],
+                src_ref=mine,
                 dst_ref=out_ref.at[gx],
                 send_sem=ss3.at[k],
                 recv_sem=sr3.at[k],
@@ -255,6 +319,7 @@
         third[-1].start()
     for copy in first + second:
         copy.wait_send()
+    keep.wait()
     for copy in third:
         copy.wait()
 
@@ -275,8 +340,8 @@
     turbines,
     total_x,
     total_y,
-    hub_ref,
-    samp_ref,
+    flat_hbm,
+    hubs_ref,
     table_ref,
     solid_hbm,
     pops_hbm,
@@ -288,6 +353,8 @@
     solid,
     force,
     field,
+    flat,
+    hub_ref,
     sems,
     out_sems,
 ):
@@ -302,6 +369,10 @@
     def plane_out(x):
         return pltpu.make_async_copy(pops.at[:, x], post_hbm.at[:, x], out_sems.at[x])
 
+    flat_copy = pltpu.make_async_copy(flat_hbm, flat, sems.at[wx + 1])
+    flat_copy.start()
+    hub_copy = pltpu.make_async_copy(hubs_ref, hub_ref, sems.at[wx + 2])
+    hub_copy.start()
     solid_copy = pltpu.make_async_copy(solid_hbm, solid, sems.at[wx])
     solid_copy.start()
     for x in range(wx):
@@ -310,17 +381,20 @@
     def rows(j):
         return table_ref[j * turbines : (j + 1) * turbines]
 
-    rel = [samp_ref[c * turbines : (c + 1) * turbines] - rows(2 + c) for c in range(3)]
+    force[...] = jnp.zeros_like(force)
+    flat_copy.wait()
+    samp = unfolded(flat[...], 3 * turbines, group)
+    rel = [samp[c * turbines : (c + 1) * turbines] - rows(2 + c) for c in range(3)]
     speed = jnp.sqrt(rel[0] * rel[0] + rel[1] * rel[1] + rel[2] * rel[2] + 0.0001)
     scale = -(rows(5) * speed)
     for c in range(3):
         pfs_ref[c * turbines : (c + 1) * turbines] = scale * rel[c]
 
-    force[...] = jnp.zeros_like(force)
+    hub_copy.wait()
     reach = [float(np.float32(math.exp(-((d / kernel_scale) ** 2)))) for d in range(SMEAR + 1)]
 
     def one_turbine(t, carry):
-        hub = hub_ref[t]
+        hub = hub_ref[t, 0]
 
         @pl.when(lax.rem(hub - start_x + SMEAR + total_x, total_x) < wx + 2 * SMEAR)
         def _():
@@ -459,7 +533,26 @@
 
 
 def stream_kernel(
-    post_hbm, from_w, from_e, from_s, from_n, from_c, out_hbm, held, rows, outs, sems, out_sems
+    turbines,
+    pack_ref,
+    rank_ref,
+    pfs_ref,
+    post_hbm,
+    from_w,
+    from_e,
+    from_s,
+    from_n,
+    from_c,
+    out_hbm,
+    pf_ref,
+    held,
+    rows,
+    sides,
+    corners,
+    outs,
+    sems,
+    edge_sems,
+    out_sems,
 ):
     wx = post_hbm.shape[1]
     wy, nz = post_hbm.shape[2:]
@@ -473,19 +566,47 @@
     for x in range(wx):
         plane_in(x).start()
     edge = 8
+    edges = []
     for j, k in enumerate(EAST):
-        held[k, 0] = from_w[j]
+        edges.append((from_w.at[j], held.at[k, 0]))
     for j, k in enumerate(WEST):
-        held[k, wx + 1] = from_e[j]
-    for ids, src, at in ((NORTH, from_s, 0), (SOUTH, from_n, 5)):
+        edges.append((from_e.at[j], held.at[k, wx + 1]))
+    edges += [(from_s, sides.at[0]), (from_n, sides.at[1]), (from_c, corners)]
+    edges = [
+        pltpu.make_async_copy(src, dst, edge_sems.at[n]) for n, (src, dst) in enumerate(edges)
+    ]
+    for copy in edges:
+        copy.start()
+
+    group = pfs_ref.shape[1]
+    data = jnp.concatenate(split3(pfs_ref[...]), axis=0).astype(bf16)
+    n_rows = 3 * turbines
+
+    def chunk(k, carry):
+        cols = pl.ds(pl.multiple_of(k * SORT_CHUNK, SORT_CHUNK), SORT_CHUNK)
+        mine = pack_ref[0:1, cols] == iota((turbines, SORT_CHUNK), 0).astype(f32)
+        place = (rank_ref[:, cols] == iota((group, SORT_CHUNK), 0).astype(f32)).astype(f32)
+        got = jnp.dot(data, place.astype(bf16), preferred_element_type=f32)
+        got = got[:n_rows] + got[n_rows : 2 * n_rows] + got[2 * n_rows :]
+        for c in range(3):
+            pf_ref[c : c + 1, cols] = jnp.sum(
+                jnp.where(mine, got[c * turbines : (c + 1) * turbines], 0.0), axis=0, keepdims=True
+            )
+        return carry
+
+    lax.fori_loop(0, pack_ref.shape[1] // SORT_CHUNK, chunk, 0)
+
+    for copy in edges:
+        copy.wait()
+    for ids, side, at in ((NORTH, 0, 0), (SOUTH, 1, 5)):
         for j, k in enumerate(ids):
-            rows[at + j, edge : edge + wx, :] = src[j]
+            rows[at + j, edge : edge + wx, :] = sides[side, j]
             if k in CORNERS:
                 n = CORNERS.index(k)
                 if lattice_dirs[k][0] == 1:
-                    rows[at + j, edge - 1 : edge, :] = from_c[n, wx - 1 : wx, :]
+                    rows[at + j, edge - 1 : edge, :] = corners[n, wx - 1 : wx, :]
                 else:
-                    rows[at + j, edge + wx : edge + wx + 1, :] = from_c[n, 0:1, :]
+                    rows[at + j, edge + wx : edge + wx + 1, :] = corners[n, 0:1, :]
     plane_in(0).wait()
     row_at = iota((wy, nz), 0)
     lane_at = iota((wy, nz), 1)
@@ -521,27 +642,6 @@
         plane_out(x).wait()
 
 
-def unsort_kernel(turbines, turb_ref, rank_ref, pfs_ref, out_ref):
-    group = pfs_ref.shape[1]
-    points = turb_ref.shape[1]
-    data = jnp.concatenate(split3(pfs_ref[...]), axis=0).astype(bf16)
-    n = 3 * turbines
-
-    def chunk(k, carry):
-        cols = pl.ds(pl.multiple_of(k * SORT_CHUNK, SORT_CHUNK), SORT_CHUNK)
-        mine = turb_ref[:, cols] == iota((turbines, SORT_CHUNK), 0)
-        place = (rank_ref[:, cols] == iota((group, SORT_CHUNK), 0).astype(f32)).astype(f32)
-        got = jnp.dot(data, place.astype(bf16), preferred_element_type=f32)
-        got = got[:n] + got[n : 2 * n] + got[2 * n :]
-        for c in range(3):
-            out_ref[c : c + 1, cols] = jnp.sum(
-                jnp.where(mine, got[c * turbines : (c + 1) * turbines], 0.0), axis=0, keepdims=True
-            )
-        return carry
-
-    lax.fori_loop(0, points // SORT_CHUNK, chunk, 0)
-
-
 def body(populations, solid_flags, point_cells, point_turbine, blade_speed, chord, turbine_gain):
     wx, wy, nz = populations.shape[1:]
     nx, ny = lax.axis_size("gx"), lax.axis_size("gy")
@@ -550,50 +650,51 @@
     group = points // turbines
     vmem = pl.BlockSpec(memory_space=pltpu.VMEM)
     smem = pl.BlockSpec(memory_space=pltpu.SMEM)
-    hbm = pl.BlockSpec(memory_space=pl.ANY)
+    hbm = pl.BlockSpec(memory_space=pltpu.HBM)
     shape = jax.ShapeDtypeStruct
     params = pltpu.CompilerParams(vmem_limit_bytes=VLIM)
-    onehot = point_turbine[None, :] == jnp.arange(turbines, dtype=jnp.int32)[:, None]
-    hubs = jnp.max(jnp.where(onehot, point_cells[0][None, :], 0), axis=1)
-    turb = point_turbine.reshape(1, points)
     dma = pltpu.SemaphoreType.DMA
-    per = -(-3 * turbines // (8 * nx)) * 8
-
-    samples, table, rank = pl.pallas_call(
+    pack = jnp.stack(
+        [point_turbine.astype(f32)]
+        + [point_cells[d].astype(f32) for d in range(3)]
+        + [blade_speed[d] for d in range(3)]
+        + [chord]
+    )
+    flat_rows = fold_sizes(3 * turbines, group)[2]
+    per = -(-flat_rows // (8 * nx)) * 8
+
+    flat, table, rank, hubs = pl.pallas_call(
         functools.partial(sample_kernel, turbines),
         out_shape=(
-            shape((nx, per, group), f32),
+            shape((nx * per, LANES), f32),
             shape((6 * turbines, group), f32),
             shape((1, points), f32),
+            shape((turbines, LANES), jnp.int32),
         ),
-        in_specs=[smem, vmem, vmem, vmem, vmem, vmem, hbm],
-        out_specs=(vmem, vmem, vmem),
+        in_specs=[smem, vmem, hbm],
+        out_specs=(hbm, vmem, vmem, vmem),
         scratch_shapes=[
             pltpu.VMEM(populations.shape, f32),
             pltpu.VMEM((15 * turbines, group), f32),
-            dma((wx,)),
+            pltpu.VMEM((3 * turbines, group), f32),
+            pltpu.VMEM((nx * per, LANES), f32),
+            pltpu.SMEM((turbines, LANES), jnp.int32),
+            dma((wx + 1,)),
         ],
         compiler_params=params,
         name="sample",
-    )(
-        hubs,
-        point_cells,
-        turb,
-        blade_speed,
-        chord.reshape(1, points),
-        turbine_gain.reshape(turbines, 1),
-        populations,
-    )
+    )(turbine_gain, pack, populations)
 
     summed = pl.pallas_call(
         functools.partial(reduce_kernel, nx, ny),
-        out_shape=shape((nx, per, group), f32),
-        in_specs=[vmem],
-        out_specs=vmem,
+        out_shape=shape((nx, per, LANES), f32),
+        in_specs=[hbm],
+        out_specs=hbm,
         scratch_shapes=[
-            pltpu.VMEM((nx, per, group), f32),
-            pltpu.VMEM((ny, per, group), f32),
-            pltpu.VMEM((per, group), f32),
+            pltpu.VMEM((per, LANES), f32),
+            pltpu.VMEM((nx, per, LANES), f32),
+            pltpu.VMEM((ny, per, LANES), f32),
+            pltpu.VMEM((per, LANES), f32),
             dma((nx,)),
             dma((nx,)),
             dma((ny,)),
@@ -603,7 +704,7 @@
         ],
         compiler_params=pltpu.CompilerParams(collective_id=0, has_side_effects=True),
         name="reduce",
-    )(samples)
+    )(flat.reshape(nx, per, LANES))
 
     pfs, north, south, post = pl.pallas_call(
         functools.partial(collide_kernel, turbines, wx * nx, wy * ny),
@@ -613,19 +714,21 @@
             shape((5, wx, nz), f32),
             shape(populations.shape, f32),
         ),
-        in_specs=[smem, vmem, vmem, hbm, hbm],
+        in_specs=[hbm, vmem, vmem, hbm, hbm],
         out_specs=(vmem, vmem, vmem, hbm),
         scratch_shapes=[
             pltpu.VMEM(populations.shape, f32),
             pltpu.VMEM((wx, wy, nz), jnp.int32),
             pltpu.VMEM((3, wx, wy, nz), f32),
             pltpu.VMEM((3 * wy, nz), f32),
-            dma((wx + 1,)),
+            pltpu.VMEM((nx * per, LANES), f32),
+            pltpu.SMEM((turbines, LANES), jnp.int32),
+            dma((wx + 3,)),
             dma((wx,)),
         ],
         compiler_params=params,
         name="collide",
-    )(hubs, summed.reshape(nx * per, group), table, solid_flags, populations)
+    )(summed.reshape(nx * per, LANES), hubs, table, solid_flags, populations)
 
     halos = pl.pallas_call(
         functools.partial(halo_kernel, nx, ny, wx),
@@ -636,38 +739,31 @@
             shape((5, wx, nz), f32),
             shape((4, wx, nz), f32),
         ),
-        in_specs=[hbm, vmem, vmem],
-        out_specs=(vmem,) * 5,
+        in_specs=[hbm, hbm, hbm],
+        out_specs=(hbm,) * 5,
         scratch_shapes=[dma((16,)), dma((16,))],
         compiler_params=pltpu.CompilerParams(collective_id=1, has_side_effects=True),
         name="halo",
     )(post, north, south)
 
-    out = pl.pallas_call(
-        stream_kernel,
-        out_shape=shape(populations.shape, f32),
-        in_specs=[hbm] + [vmem] * 5,
-        out_specs=hbm,
+    return pl.pallas_call(
+        functools.partial(stream_kernel, turbines),
+        out_shape=(shape(populations.shape, f32), shape((3, points), f32)),
+        in_specs=[vmem] * 3 + [hbm] * 6,
+        out_specs=(hbm, vmem),
         scratch_shapes=[
             pltpu.VMEM((NDIR, wx + 2, wy, nz), f32),
             pltpu.VMEM((10, wx + 16, nz), f32),
+            pltpu.VMEM((2, 5, wx, nz), f32),
+            pltpu.VMEM((4, wx, nz), f32),
             pltpu.VMEM(populations.shape, f32),
             dma((wx,)),
+            dma((13,)),
             dma((wx,)),
         ],
-        compiler_params=params,
+        compiler_params=pltpu.CompilerParams(vmem_limit_bytes=STREAM_VLIM),
         name="stream",
-    )(post, *halos)
-
-    point_force = pl.pallas_call(
-        functools.partial(unsort_kernel, turbines),
-        out_shape=shape((3, points), f32),
-        in_specs=[vmem, vmem, vmem],
-        out_specs=vmem,
-        compiler_params=params,
-        name="unsort",
-    )(turb, rank, pfs)
-    return out, point_force
+    )(pack, rank, pfs, post, *halos)
 
 
 def solution(mesh):

time: 73.8 us -> 59.8 us (0.81); the launches traced: 72.7 us -> 60.3 us
  local copies, waits for them, and re-layouts: 18.8 us -> 2.46 us
  Pallas kernels: 52.3 us -> 55.4 us
  other arithmetic: 0.9 us -> 1.78 us
    unnamed x30 -> x0, local copies, waits for them, and re-layouts: 15.6 us -> none
    pallas_call x1, Pallas kernels: 8.05 us -> 11.9 us  [body(): pl.pallas_call(functools.partial(collide_kernel, turbines, wx * nx, wy *...]
    pallas_call x1, Pallas kernels: 21.3 us -> 17.8 us  [body(): pl.pallas_call(functools.partial(reduce_kernel, nx, ny), out_shape=shape(...]
    another operation x0 -> x3, local copies, waits for them, and re-layouts: none -> 2.46 us  [body(): jnp.stack([point_turbine.astype(f32)] + [point_cells[d].astype(f32) for d...]
    pallas_call x1, Pallas kernels: 4.74 us -> 6.7 us  [body(): pl.pallas_call(functools.partial(sample_kernel, turbines), out_shape=(sha...]
    convert_element_type x0 -> x2, other arithmetic: none -> 1.78 us  [the longest x1 1.05 us: body(): point_cells[d].astype(f32)]
    reshape x2 -> x0, local copies, waits for them, and re-layouts: 1.48 us -> none  [the longest x1 0.74 us: body(): chord.reshape(1, points)]
    pallas_call x2 -> x1, Pallas kernels: 5.84 us -> 6.79 us  [body(): pl.pallas_call(functools.partial(stream_kernel, turbines), out_shape=(sha...]
where the time goes in v1:
time: 59.8 us; the launch traced here: 60.3 us
  Pallas kernels  55.4 us (93%)
  local copies, waits for them, and re-layouts  2.46 us (4%)
  other arithmetic  1.78 us (3%)
  between operations  0.67 us (1%)
    pallas_call x1, Pallas kernels, body(): pl.pallas_call(functools.partial(reduce_kernel, nx, ny), out_shape=shape(...  17.8 us
    pallas_call x1, Pallas kernels, body(): pl.pallas_call(functools.partial(halo_kernel, nx, ny, wx), out_shape=(sha...  12.3 us
    pallas_call x1, Pallas kernels, body(): pl.pallas_call(functools.partial(collide_kernel, turbines, wx * nx, wy *...  11.9 us
    pallas_call x1, Pallas kernels, body(): pl.pallas_call(functools.partial(stream_kernel, turbines), out_shape=(sha...  6.79 us
    pallas_call x1, Pallas kernels, body(): pl.pallas_call(functools.partial(sample_kernel, turbines), out_shape=(sha...  6.7 us
    another operation x3, local copies, waits for them, and re-layouts, body(): jnp.stack([point_turbine.astype(f32)] + [point_cells[d].astype(f32) for d...  2.46 us

profile of v1, /device:TPU:0, one launch (start us, length us, event | category | flops | bytes accessed | tf_op | source)
XLA Modules:
  0.0 60.3 jit_solution(12349535091068762258)
XLA Ops:
  0.6 0.7 %stack.13 = f32[1,4608]{1,0:T(1,128)S(1)} reshape(f32[4608]{0:T(1024)} %param.12) | data formatting | bytes 36864 | tf_op jit(solution)/shard_map/stack | solution.py:657
  1.4 0.7 %convert_element_type.15 = f32[4608]{0:T(1024)S(1)} convert(s32[4608]{0:T(1024)} %param.10) | non-fusion elementwise | flops 4608 | bytes 36864 | tf_op jit(solution)/shard_map/convert_element_type | solution.py:658
  2.1 1.1 %slice_convert_fusion = (f32[1,4608]{1,0:T(1,128)S(1)}, f32[1,4608]{1,0:T(1,128)S(1)}, f32[1,4608]{1,0:T(1,128)S(1)}) fusion(s32[3,4608]{1,0:T(4,128)} %param.9), kind=kLoop, calls=%fused_computation | loop fusion | flops 13824 | bytes 110592 | tf_op jit(solution)/shard_map/convert_element_type | solution.py:659
  3.2 1.7 %stack.14.pack_ref = f32[8,4608]{1,0:T(8,128)} concatenate(f32[1,4608]{1,0:T(1,128)S(1)} %stack.12, f32[1,4608]{1,0:T(1,128)S(1)} %get-tuple-element.29, f32[1,4608]{1,0:T(1,128)S(1)} %get-tuple-element.30, f32[1,4608]{1,0:T(1,128)S(1)} %get-tuple-element.28, f32[3,4608]{1,0:T(4,128)} %param.11, f32[1,4608]{1,0:T(1,128)S(1)} %stack.13), dimensions={0} | concatenate | bytes 294912 | tf_op jit(solution)/shard_map/stack | solution.py:657
  4.9 6.7 %sample.1 = (f32[128,128]{1,0:T(8,128)}, f32[144,192]{1,0:T(8,128)}, f32[1,4608]{1,0:T(1,128)}, s32[24,128]{1,0:T(8,128)}) custom-call(f32[24]{0:T(128)} %gain_ref.1, f32[8,4608]{1,0:T(8,128)} %stack.14.pack_ref, f32[19,8,64,128]{3,2,1,0:T(8,128)} %pops_hbm.3), custom_call_target="tpu_custom_call" | custom-call | tf_op jit(solution)/shard_map/sample/pallas_call | solution.py:666
  11.6 17.8 %reduce.1 = f32[8,16,128]{2,1,0:T(8,128)} custom-call(f32[8,16,128]{2,1,0:T(8,128)} %bitcast.3), custom_call_target="tpu_custom_call" | custom-call | tf_op jit(solution)/shard_map/reduce/pallas_call | solution.py:688
  29.4 11.9 %collide.1 = (f32[72,192]{1,0:T(8,128)}, f32[5,8,128]{2,1,0:T(8,128)}, f32[5,8,128]{2,1,0:T(8,128)}, f32[19,8,64,128]{3,2,1,0:T(8,128)}) custom-call(f32[128,128]{1,0:T(8,128)} %bitcast.2, s32[24,128]{1,0:T(8,128)} %get-tuple-element.17.hubs_ref, f32[144,192]{1,0:T(8,128)} %get-tuple-element.18.table_ref, s32[8,64,128]{2,1,0:T(8,128)} %solid_hbm.1, ...), custom_call_target="tpu_custom_call" | custom-call | tf_op jit(solution)/shard_map/collide/pallas_call | solution.py:709
  41.2 12.3 %halo.1 = (f32[5,64,128]{2,1,0:T(8,128)}, f32[5,64,128]{2,1,0:T(8,128)}, f32[5,8,128]{2,1,0:T(8,128)}, f32[5,8,128]{2,1,0:T(8,128)}, f32[4,8,128]{2,1,0:T(8,128)}) custom-call(f32[19,8,64,128]{3,2,1,0:T(8,128)} %get-tuple-element.20.post.post_hbm, f32[5,8,128]{2,1,0:T(8,128)} %get-tuple-element.21.north, f32[5,8,128]{2,1,0:T(8,128)} %get-tuple-element.22.south), custom_call_target="tpu_custom_call" | custom-call | tf_op jit(solution)/shard_map/halo/pallas_call | solution.py:733
  53.6 6.8 %stream.1 = (f32[19,8,64,128]{3,2,1,0:T(8,128)}, f32[3,4608]{1,0:T(4,128)}) custom-call(f32[8,4608]{1,0:T(8,128)} %stack.14.pack_ref, f32[1,4608]{1,0:T(1,128)} %get-tuple-element.15.rank_ref, f32[72,192]{1,0:T(8,128)} %get-tuple-element.19.pfs_ref, f32[19,8,64,128]{3,2,1,0:T(8,128)} %get-tuple-element.20.post.post_hbm, ...), custom_call_target="tpu_custom_call" | custom-call | tf_op jit(solution)/shard_map/stream/pallas_call | solution.py:749
  (1 shorter events, 0.0 us)
